TPU v7x, 1024 devices: a whole 8x8x8 slice. The times are simulated.
1024 devices in a mesh: tok: 8 (over z), row: 8 (over x), col: 16 (over y, core).
Axes of the slice: x: 8, y: 8, z: 8, core: 2. Of those that a mesh axis runs over, the one named last changes fastest.
Arguments:
- tokens: bfloat16 [1024, 8192], P('tok', 'row'), may hold values from -6 to 6
- w1_blocks: bfloat16 [8, 16, 8, 128, 128], P('row', 'col'), may hold values from -0.25 to 0.25
- w1_rows: int32 [8, 16, 8], P('row', 'col'), may hold values from 0 to 7
- w1_cols: int32 [8, 16, 8], P('row', 'col'), may hold values from 0 to 15
- w2_blocks: bfloat16 [8, 16, 8, 128, 128], P('row', 'col'), may hold values from -0.125 to 0.125
- w2_hidden: int32 [8, 16, 8], P('row', 'col'), may hold values from 0 to 15
- w2_outs: int32 [8, 16, 8], P('row', 'col'), may hold values from 0 to 7
- grad_out: bfloat16 [1024, 8192], P('tok', 'row'), may hold values from -6 to 6
Outputs:
- output: bfloat16 [1024, 8192], P(('tok', 'col'), 'row')
- grad_in: bfloat16 [1024, 8192], P(('tok', 'col'), 'row')
- grad_w1: float32 [8, 16, 8, 128, 128], P('row', 'col', None, 'tok')
- grad_w2: float32 [8, 16, 8, 128, 128], P('row', 'col', None, 'tok')
All inputs are finite; a program needn't handle non-finite values.
Results may differ from a plain program's by a relative error of at most 0.0049.
Values may be sent and summed in bfloat16 or wider, within the bound.
A program may use at most 32 MiB of HBM per device.

v0:
```python
import jax
import jax.numpy as jnp
from jax import lax
from jax.sharding import PartitionSpec as P

FF = 32768


highest = lax.Precision.HIGHEST


def gelu_value(value):
    return value * (0.5 * (1.0 + jax.scipy.special.erf(value / jnp.sqrt(2.0))))


def gelu_slope(value):
    cdf_part = 0.5 * (1.0 + jax.scipy.special.erf(value / jnp.sqrt(2.0)))
    return cdf_part + value * jnp.exp(-0.5 * value * value) / jnp.sqrt(2.0 * jnp.pi)


def select_blocks(source, indices, count):
    block = source.shape[1] // count
    onehot = (indices[:, None] == jnp.arange(count, dtype=jnp.int32)[None, :]).astype(jnp.bfloat16)
    shaped = source.reshape(source.shape[0], count, block)
    taken = jnp.einsum("kr,trb->ktb", onehot, shaped, preferred_element_type=jnp.float32)
    return taken.astype(jnp.bfloat16)


def place_blocks(product, indices, count):
    onehot = (indices[:, None] == jnp.arange(count, dtype=jnp.int32)[None, :]).astype(jnp.float32)
    placed = jnp.einsum("kc,ktj->tcj", onehot, product, precision=highest)
    return placed.reshape(product.shape[1], count * product.shape[2])


def apply_blocks(taken, weights, index_out, count_out, flip):
    form = "ktb,kjb->ktj" if flip else "ktb,kbj->ktj"
    product = jnp.einsum(form, taken, weights, preferred_element_type=jnp.float32)
    return place_blocks(product, index_out, count_out)


def shards(tokens, w1_blocks, w1_rows, w1_cols, w2_blocks, w2_hidden, w2_outs, grad_out):
    slots = w1_blocks.shape[2]
    block = w1_blocks.shape[-1]
    row_blocks = tokens.shape[1] // block
    col_blocks = FF // lax.axis_size("col") // block
    first = w1_blocks.reshape(slots, block, block)
    second = w2_blocks.reshape(slots, block, block)
    first_rows = w1_rows.reshape(slots)
    first_cols = w1_cols.reshape(slots)
    second_hidden = w2_hidden.reshape(slots)
    second_outs = w2_outs.reshape(slots)
    share_rows = tokens.shape[0] // lax.axis_size("row")
    token_taken = select_blocks(tokens, first_rows, row_blocks)
    partial_value = apply_blocks(token_taken, first, first_cols, col_blocks, False)
    hidden = lax.psum(partial_value, "row")
    active = gelu_value(hidden).astype(jnp.bfloat16)
    start = lax.axis_index("row") * share_rows
    hidden_part = lax.dynamic_slice_in_dim(hidden, start, share_rows, 0)
    active_taken = select_blocks(active, second_hidden, col_blocks)
    out_part = apply_blocks(active_taken, second, second_outs, row_blocks, False)
    output = lax.psum_scatter(out_part, "col", scatter_dimension=0, tiled=True).astype(jnp.bfloat16)
    cotangent_taken = select_blocks(grad_out, second_outs, row_blocks)
    back_part = apply_blocks(cotangent_taken, second, second_hidden, col_blocks, True)
    back_part_sum = lax.psum_scatter(back_part, "row", scatter_dimension=0, tiled=True)
    grad_part = (back_part_sum * gelu_slope(hidden_part)).astype(jnp.bfloat16)
    grad_hidden = lax.all_gather(grad_part, "row", axis=0, tiled=True)
    grad_taken = select_blocks(grad_hidden, first_cols, col_blocks)
    input_part = apply_blocks(grad_taken, first, first_rows, row_blocks, True)
    grad_in = lax.psum_scatter(input_part, "col", scatter_dimension=0, tiled=True).astype(
        jnp.bfloat16
    )
    first_grad = jnp.einsum(
        "ktb,ktj->kbj", token_taken, grad_taken, preferred_element_type=jnp.float32
    )
    second_grad = jnp.einsum(
        "ktb,ktj->kbj", active_taken, cotangent_taken, preferred_element_type=jnp.float32
    )
    summed = (
        lax.psum_scatter(
            first_grad.reshape(1, 1, slots, block, block), "tok", scatter_dimension=3, tiled=True
        ),
        lax.psum_scatter(
            second_grad.reshape(1, 1, slots, block, block), "tok", scatter_dimension=3, tiled=True
        ),
    )
    return (output, grad_in, summed[0], summed[1])


def solution(mesh):
    placed = (
        P("tok", "row"),
        P("row", "col", None, None, None),
        P("row", "col", None),
        P("row", "col", None),
        P("row", "col", None, None, None),
        P("row", "col", None),
        P("row", "col", None),
        P("tok", "row"),
    )
    return jax.shard_map(
        shards,
        mesh=mesh,
        in_specs=placed,
        out_specs=(
            P(("tok", "col"), "row"),
            P(("tok", "col"), "row"),
            P("row", "col", None, "tok", None),
            P("row", "col", None, "tok", None),
        ),
        check_vma=False,
    )
```

profile of v0, /device:TPU:1, one launch (start us, length us, event | category | flops | bytes accessed | tf_op | source)
XLA Modules:
  0.0 385.5 jit_solution(11867433465461217644)
XLA Ops:
  7.2 0.0 all-reduce.2.cloned.1.call-start
  7.2 1.0 copy.28
  8.3 0.6 copy-done.4
  8.9 0.3 convolution_convert_fusion.3
  9.2 0.2 copy.14
  9.4 0.7 copy-done.1
  10.1 0.3 fusion.15
  10.4 0.6 copy-done.6
  11.1 0.9 fusion.6
  11.9 1.3 copy.57
  13.3 0.0 all-reduce.2.cloned.1.call-update
  13.3 0.0 reduce-scatter.8.cloned.1.call-start
  13.4 0.9 copy-done.2
  14.3 0.6 copy-done.3
  14.9 0.3 convolution_convert_fusion.2
  15.2 0.3 fusion.9
  15.5 0.6 copy-done.5
  16.2 0.9 fusion.2
  17.0 1.4 copy.56
  18.4 0.0 reduce-scatter.8.cloned.1.call-update
  18.4 0.0 reduce-scatter.6.cloned.1.call-start
  18.5 89.8 %all-reduce.2.cloned.1.call-done = f32[128,2048]{1,0:T(8,128)} async-done(((f32[128,2048]{1,0:T(8,128)}), f32[128,2048]{1,0:T(8,128)}) %all-reduce.2.cloned.1.call-update) | async-done | bytes 1048592 | tf_op jit(solution)/shard_map/psum | solution.py:55
  108.2 1.5 fusion.8
  109.7 0.1 copy.30
  109.8 0.3 convolution_convert_fusion.1
  110.1 0.2 copy.16
  110.3 0.3 fusion.11
  110.6 0.7 fusion.4
  111.4 0.9 copy.59
  112.3 0.0 reduce-scatter.10.cloned.1.call-start
  112.3 42.3 %reduce-scatter.8.cloned.1.call-done = f32[16,2048]{1,0:T(8,128)} async-done(((f32[128,2048]{1,0:T(8,128)}), f32[16,2048]{1,0:T(8,128)}) %reduce-scatter.8.cloned.1.call-update) | async-done | bytes 131088 | tf_op jit(solution)/shard_map/reduce_scatter | solution.py:64
  154.6 1.0 fusion.26
  155.6 19.4 %all_gather.3 = bf16[128,2048]{1,0:T(8,128)(2,1)S(1)} all-gather(bf16[16,2048]{1,0:T(8,128)(2,1)S(1)} %fusion.26), channel_id=1, replica_groups=mesh['tok'=8,'row'=8,'col'=16] {'row'}, dimensions={0}, use_global_device_ids=true | all-gather | bytes 589824 | tf_op jit(solution)/shard_map/all_gather | solution.py:66
  175.1 0.1 copy.34
  175.2 0.3 convolution_convert_fusion
  175.5 0.3 fusion.13
  175.8 0.7 fusion
  176.4 0.9 copy.58
  177.3 0.0 reduce-scatter.14.cloned.1.call-start
  177.4 1.0 convolution_bitcast_fusion
  178.5 0.0 reduce-scatter.12.cloned.1.call-start
  178.5 1.0 convolution_bitcast_fusion.1
  179.5 44.0 %reduce-scatter.6.cloned.1.call-done = f32[8,1024]{1,0:T(8,128)} async-done(((f32[128,1024]{1,0:T(8,128)}), f32[8,1024]{1,0:T(8,128)}) %reduce-scatter.6.cloned.1.call-update) | async-done | bytes 32784 | tf_op jit(solution)/shard_map/reduce_scatter | solution.py:61
  223.6 1.4 convert_element_type.35
  224.9 63.3 %reduce-scatter.10.cloned.1.call-done = f32[8,1024]{1,0:T(8,128)} async-done(((f32[128,1024]{1,0:T(8,128)}), f32[8,1024]{1,0:T(8,128)}) %reduce-scatter.10.cloned.1.call-update) | async-done | bytes 32784 | tf_op jit(solution)/shard_map/reduce_scatter | solution.py:69
  288.3 1.4 convert_element_type.39
  289.6 42.5 %reduce-scatter.14.cloned.1.call-done = f32[1,1,8,16,128]{4,3,2,1,0:T(8,128)} async-done(((f32[1,1,8,128,128]{4,3,2,1,0:T(8,128)}), f32[1,1,8,16,128]{4,3,2,1,0:T(8,128)}) %reduce-scatter.14.cloned.1.call-update) | async-done | bytes 65552 | tf_op jit(solution)/shard_map/reduce_scatter | solution.py:82
  332.2 46.5 %reduce-scatter.12.cloned.1.call-done = f32[1,1,8,16,128]{4,3,2,1,0:T(8,128)} async-done(((f32[1,1,8,128,128]{4,3,2,1,0:T(8,128)}), f32[1,1,8,16,128]{4,3,2,1,0:T(8,128)}) %reduce-scatter.12.cloned.1.call-update) | async-done | bytes 65552 | tf_op jit(solution)/shard_map/reduce_scatter | solution.py:79
  (13 shorter events, 0.1 us)
Async XLA Ops:
  7.2 8.0 %copy-start = (bf16[1,1,8,128,128]{4,3,2,1,0:T(8,128)(2,1)S(1)}, bf16[1,1,8,128,128]{4,3,2,1,0:T(8,128)(2,1)}, u32[]{:S(2)}) copy-start(bf16[1,1,8,128,128]{4,3,2,1,0:T(8,128)(2,1)} %param.12) | copy-start | bytes 786436
  7.2 101.1 %all-reduce.2.cloned.1.call-start = ((), (), s32[]{:S(2)}) async-start(), calls=%async_computation.5 | async-start | bytes 2097152 | tf_op jit(solution)/shard_map/psum | solution.py:55
  8.3 0.7 copy-start.4
  9.2 1.0 copy-start.1
  10.4 0.7 copy-start.6
  13.3 0.9 copy-start.2
  13.3 141.3 %reduce-scatter.8.cloned.1.call-start = ((), (), s32[]{:S(2)}) async-start(), calls=%async_computation.7 | async-start | bytes 1179648 | tf_op jit(solution)/shard_map/reduce_scatter | solution.py:64
  14.3 0.7 copy-start.3
  15.5 0.7 copy-start.5
  18.4 205.1 %reduce-scatter.6.cloned.1.call-start = ((), (), s32[]{:S(2)}) async-start(), calls=%async_computation.6 | async-start | bytes 557056 | tf_op jit(solution)/shard_map/reduce_scatter | solution.py:61
  112.3 176.0 %reduce-scatter.10.cloned.1.call-start = ((), (), s32[]{:S(2)}) async-start(), calls=%async_computation.8 | async-start | bytes 557056 | tf_op jit(solution)/shard_map/reduce_scatter | solution.py:69
  177.3 154.8 %reduce-scatter.14.cloned.1.call-start = ((), (), s32[]{:S(2)}) async-start(), calls=%async_computation.10 | async-start | bytes 589824 | tf_op jit(solution)/shard_map/reduce_scatter | solution.py:82
  178.5 200.2 %reduce-scatter.12.cloned.1.call-start = ((), (), s32[]{:S(2)}) async-start(), calls=%async_computation.9 | async-start | bytes 589824 | tf_op jit(solution)/shard_map/reduce_scatter | solution.py:79
Sparse Core Ops, SparseCore 0:
  13.4 94.7 all-reduce.1
  111.6 42.9 reduce-scatter.7
  158.0 65.5 reduce-scatter.5
  227.2 61.0 reduce-scatter.9
  292.1 40.0 reduce-scatter.13
  336.4 42.2 reduce-scatter.11
where the time goes:
time: 389 us; the launch traced here: 385 us
  waiting for transfers between devices  328 us (84%)
  blocking collectives  19.4 us (5%)
  between operations  14.3 us (4%)
  local copies, waits for them, and re-layouts  10.4 us (3%)
  matrix products  7.38 us (2%)
  other arithmetic  5.21 us (1%)
    psum x1, waiting for transfers between devices, shards(): hidden = lax.psum(partial_value, 'row')  89.8 us
    reduce_scatter x1, waiting for transfers between devices, shards(): lax.psum_scatter(input_part, 'col', scatter_dimension=0, tiled=True)  63.3 us
    reduce_scatter x1, waiting for transfers between devices, shards(): lax.psum_scatter(first_grad.reshape(1, 1, slots, block, block), 'tok', sc...  46.5 us
    reduce_scatter x1, waiting for transfers between devices, shards(): lax.psum_scatter(out_part, 'col', scatter_dimension=0, tiled=True)  44 us
    reduce_scatter x1, waiting for transfers between devices, shards(): lax.psum_scatter(second_grad.reshape(1, 1, slots, block, block), 'tok', s...  42.5 us
    reduce_scatter x1, waiting for transfers between devices, shards(): lax.psum_scatter(back_part, 'row', scatter_dimension=0, tiled=True)  42.3 us
    all_gather x1, blocking collectives, shards(): grad_hidden = lax.all_gather(grad_part, 'row', axis=0, tiled=True)  19.4 us
    unnamed x22, local copies, waits for them, and re-layouts  9.98 us
  transfers between devices with their start and end apart: 6, of which 6 were waited for; matrix products, arithmetic and copies ran while one was open for 4% of the time, Pallas kernels for 0%

commit v1 on v0

v1 whole, which is shorter than its diff:
```python
import functools

import jax
import jax.numpy as jnp
from jax import lax
from jax.experimental import pallas as pl
from jax.experimental.pallas import tpu as pltpu
from jax.sharding import PartitionSpec as P

MESH = pl.DeviceIdType.MESH
F32 = jnp.float32
BF16 = jnp.bfloat16
INV_SQRT2 = 0.7071067811865476
INV_SQRT_2PI = 0.3989422804014327
IDX, HID, BACK, ACT, GRAD, OUT, GIN, GW2, GW1 = range(9)


def far_first(size):
    return sorted(range(1, size), key=lambda d: -min(d, size - d))


def kernel(
    size,
    rows1, cols1, hid2, outs2,
    tok_hbm, w1_hbm, w2_hbm, go_hbm,
    out_ref, gin_ref, gw1_ref, gw2_ref,
    tok_ref, w1_ref, w2_ref, go_ref,
    idx_mine, idx_all, idx_s,
    sh, rh, sb, rb, sa, ra, sg, rg,
    act, slope, prod,
    sy1, ry1, sy2, ry2,
    sz1, rz1, sz2, rz2,
    send_sem, recv_sem, in_sem, idx_sem,
):
    n_tok, n_row, n_col = size
    row_blocks, tokens, _ = tok_ref.shape
    slots, blk = w1_ref.shape[0], w1_ref.shape[2]
    col_blocks, share = act.shape[0], act.shape[1]
    t, r, c = lax.axis_index("tok"), lax.axis_index("row"), lax.axis_index("col")

    def columns(src, dst, first):
        return [
            pltpu.make_async_copy(src.at[:, b * blk : (b + 1) * blk], dst.at[b], in_sem.at[first + b])
            for b in range(row_blocks)
        ]

    first_loads = columns(tok_hbm, tok_ref, 0)
    first_loads.append(pltpu.make_async_copy(w1_hbm, w1_ref, in_sem.at[2 * row_blocks]))
    second_loads = columns(go_hbm, go_ref, row_blocks)
    second_loads.append(pltpu.make_async_copy(w2_hbm, w2_ref, in_sem.at[2 * row_blocks + 1]))
    for load in first_loads + second_loads:
        load.start()

    places = (("row", r, n_row), ("col", c, n_col), ("tok", t, n_tok))
    barrier = pltpu.get_barrier_semaphore()
    for axis, me, count in places:
        for d in far_first(count):
            pl.semaphore_signal(
                barrier, inc=1, device_id={axis: lax.rem(me + d, count)}, device_id_type=MESH
            )

    def send(axis, me, count, src, dst, phase, whole=False):
        for d in far_first(count):
            peer = lax.rem(me + d, count)
            pltpu.make_async_remote_copy(
                src_ref=src if whole else src.at[peer],
                dst_ref=dst.at[me],
                send_sem=send_sem.at[phase],
                recv_sem=recv_sem.at[phase],
                device_id={axis: peer},
                device_id_type=MESH,
            ).start()

    def wait(buf, count, sem):
        span = buf.at[pl.ds(0, count - 1)]
        pltpu.make_async_copy(span, span, sem).wait()

    def dot(a, b, ca, cb):
        return lax.dot_general(a, b, (((ca,), (cb,)), ((), ())), preferred_element_type=F32)

    for k in range(slots):
        idx_mine[pl.ds(k, 1), :] = jnp.full((1, blk), cols1[k], jnp.int32)
        idx_mine[pl.ds(slots + k, 1), :] = jnp.full((1, blk), hid2[k], jnp.int32)
    idx_all[r] = idx_mine[...]

    for load in first_loads:
        load.wait()
    for k in range(slots):
        p = dot(tok_ref[rows1[k]], w1_ref[k], 1, 0)
        sh[:, k] = p.astype(BF16).reshape(n_row, share, blk)
    rh[r] = sh[r]
    for load in second_loads:
        load.wait()
    for k in range(slots):
        p = dot(go_ref[outs2[k]], w2_ref[k], 1, 1)
        sb[:, k] = p.astype(BF16).reshape(n_row, share, blk)
    rb[r] = sb[r]

    pl.semaphore_wait(barrier, n_row + n_col + n_tok - 3)
    send("row", r, n_row, idx_mine, idx_all, IDX, whole=True)
    send("row", r, n_row, sh, rh, HID)
    send("row", r, n_row, sb, rb, BACK)

    wait(idx_all, n_row, recv_sem.at[IDX])
    to_smem = pltpu.make_async_copy(idx_all, idx_s, idx_sem)
    to_smem.start()
    to_smem.wait()

    places_of_block = lax.broadcasted_iota(jnp.int32, (col_blocks, share, blk), 0)

    def place(buf, first):
        def body(s, total):
            q, k = s // slots, s % slots
            where = idx_all[q, pl.ds(first + k, 1), :]
            hit = places_of_block == where[None]
            return total + jnp.where(hit, buf[q, k].astype(F32)[None], 0.0)

        return lax.fori_loop(
            0, n_row * slots, body, jnp.zeros((col_blocks, share, blk), F32)
        )

    def gather(dst, first):
        def body(s, carry):
            q, k = s // slots, s % slots
            dst[q, k] = act[idx_s[q, first + k, 0]]
            return carry

        lax.fori_loop(0, n_row * slots, body, 0)

    wait(rh, n_row, recv_sem.at[HID])
    hidden = place(rh, 0)
    cdf = 0.5 * (1.0 + lax.erf(hidden * INV_SQRT2))
    act[...] = (hidden * cdf).astype(BF16)
    slope[...] = cdf + hidden * jnp.exp(-0.5 * hidden * hidden) * INV_SQRT_2PI
    gather(sa, slots)
    ra[r] = sa[r]
    send("row", r, n_row, sa, ra, ACT)

    wait(rb, n_row, recv_sem.at[BACK])
    act[...] = (place(rb, slots) * slope[...]).astype(BF16)
    gather(sg, 0)
    rg[r] = sg[r]
    send("row", r, n_row, sg, rg, GRAD)

    def scatter_out(index, dst):
        half = row_blocks // 2
        own = tokens // n_col

        def total(b):
            acc = jnp.zeros((tokens, blk), F32)
            for k in range(slots):
                hit = jnp.full((tokens, blk), index[k], jnp.int32) == b
                acc += jnp.where(hit, prod[k], 0.0)
            return acc.reshape(n_col, own, blk)

        for b in range(half):
            both = jnp.concatenate([total(b), total(b + half)], axis=1)
            dst[:, :, b * blk : (b + 1) * blk] = both.astype(BF16)

    wait(ra, n_row, recv_sem.at[ACT])
    for k in range(slots):
        prod[k] = dot(ra[:, k].reshape(tokens, blk), w2_ref[k], 1, 0)
    scatter_out(outs2, sy1)
    ry1[c] = sy1[c]
    send("col", c, n_col, sy1, ry1, OUT)
    for k in range(slots):
        p = dot(ra[:, k].reshape(tokens, blk), go_ref[outs2[k]], 0, 0)
        sz2[:, k] = p.astype(BF16).reshape(n_tok, blk // n_tok, blk)
    rz2[t] = sz2[t]
    send("tok", t, n_tok, sz2, rz2, GW2)

    wait(rg, n_row, recv_sem.at[GRAD])
    for k in range(slots):
        prod[k] = dot(rg[:, k].reshape(tokens, blk), w1_ref[k], 1, 1)
    scatter_out(rows1, sy2)
    ry2[c] = sy2[c]
    send("col", c, n_col, sy2, ry2, GIN)
    for k in range(slots):
        p = dot(tok_ref[rows1[k]], rg[:, k].reshape(tokens, blk), 0, 0)
        sz1[:, k] = p.astype(BF16).reshape(n_tok, blk // n_tok, blk)
    rz1[t] = sz1[t]
    send("tok", t, n_tok, sz1, rz1, GW1)

    def finish_rows(buf, out):
        own = out.shape[0]
        half = out.shape[1] // 2
        total = jnp.sum(buf[...].astype(F32), axis=0).astype(BF16)
        out[:, :half] = total[:own]
        out[:, half:] = total[own:]

    wait(ry1, n_col, recv_sem.at[OUT])
    finish_rows(ry1, out_ref)
    wait(rz2, n_tok, recv_sem.at[GW2])
    gw2_ref[...] = jnp.sum(rz2[...].astype(F32), axis=0)
    wait(ry2, n_col, recv_sem.at[GIN])
    finish_rows(ry2, gin_ref)
    wait(rz1, n_tok, recv_sem.at[GW1])
    gw1_ref[...] = jnp.sum(rz1[...].astype(F32), axis=0)

    wait(idx_all, n_row, send_sem.at[IDX])
    for buf, count, phase in (
        (sh, n_row, HID), (sb, n_row, BACK), (sa, n_row, ACT), (sg, n_row, GRAD),
        (sy1, n_col, OUT), (sy2, n_col, GIN), (sz2, n_tok, GW2), (sz1, n_tok, GW1),
    ):
        wait(buf, count, send_sem.at[phase])


def shards(size, hidden_width, tokens, w1_blocks, w1_rows, w1_cols, w2_blocks, w2_hidden, w2_outs, grad_out):
    n_tok, n_row, n_col = size
    slots, blk = w1_blocks.shape[2], w1_blocks.shape[-1]
    rows, width = tokens.shape
    col_blocks = hidden_width // n_col // blk
    share, own, strip = rows // n_row, rows // n_col, blk // n_tok
    any_spec = pl.BlockSpec(memory_space=pl.ANY)
    smem = pl.BlockSpec(memory_space=pltpu.SMEM)
    vmem = pl.BlockSpec(memory_space=pltpu.VMEM)
    along_row = pltpu.VMEM((n_row, slots, share, blk), BF16)
    along_col = pltpu.VMEM((n_col, 2 * own, width // 2), BF16)
    along_tok = pltpu.VMEM((n_tok, slots, strip, blk), BF16)
    out, gin, gw1, gw2 = pl.pallas_call(
        functools.partial(kernel, size),
        out_shape=(
            jax.ShapeDtypeStruct((own, width), BF16),
            jax.ShapeDtypeStruct((own, width), BF16),
            jax.ShapeDtypeStruct((slots, strip, blk), F32),
            jax.ShapeDtypeStruct((slots, strip, blk), F32),
        ),
        in_specs=[smem] * 4 + [any_spec] * 4,
        out_specs=[vmem] * 4,
        scratch_shapes=[
            pltpu.VMEM((width // blk, rows, blk), BF16),
            pltpu.VMEM((slots, blk, blk), BF16),
            pltpu.VMEM((slots, blk, blk), BF16),
            pltpu.VMEM((width // blk, rows, blk), BF16),
            pltpu.VMEM((2 * slots, blk), jnp.int32),
            pltpu.VMEM((n_row, 2 * slots, blk), jnp.int32),
            pltpu.SMEM((n_row, 2 * slots, blk), jnp.int32),
        ]
        + [along_row] * 8
        + [
            pltpu.VMEM((col_blocks, share, blk), BF16),
            pltpu.VMEM((col_blocks, share, blk), F32),
            pltpu.VMEM((slots, rows, blk), F32),
        ]
        + [along_col] * 4
        + [along_tok] * 4
        + [
            pltpu.SemaphoreType.DMA((9,)),
            pltpu.SemaphoreType.DMA((9,)),
            pltpu.SemaphoreType.DMA((2 * (width // blk) + 2,)),
            pltpu.SemaphoreType.DMA,
        ],
        compiler_params=pltpu.CompilerParams(collective_id=0, has_side_effects=True),
        name="block_sparse_ffn",
    )(
        w1_rows.reshape(slots), w1_cols.reshape(slots), w2_hidden.reshape(slots), w2_outs.reshape(slots),
        tokens, w1_blocks.reshape(slots, blk, blk), w2_blocks.reshape(slots, blk, blk), grad_out,
    )
    return out, gin, gw1.reshape(1, 1, slots, strip, blk), gw2.reshape(1, 1, slots, strip, blk)


def solution(mesh, hidden_width=32768):
    placed = (
        P("tok", "row"),
        P("row", "col", None, None, None),
        P("row", "col", None),
        P("row", "col", None),
        P("row", "col", None, None, None),
        P("row", "col", None),
        P("row", "col", None),
        P("tok", "row"),
    )
    size = tuple(mesh.shape[axis] for axis in ("tok", "row", "col"))
    return jax.shard_map(
        functools.partial(shards, size, hidden_width),
        mesh=mesh,
        in_specs=placed,
        out_specs=(
            P(("tok", "col"), "row"),
            P(("tok", "col"), "row"),
            P("row", "col", None, "tok", None),
            P("row", "col", None, "tok", None),
        ),
        check_vma=False,
    )
```

time: 389 us -> 63.3 us (0.16)
  the two profiles are of different devices: /device:TPU:1 before, /device:TPU:7 now
where the time goes in v1:
time: 63.3 us; the launch traced here: 63 us
  Pallas kernels  58.2 us (92%)
  local copies, waits for them, and re-layouts  4.17 us (7%)
  between operations  0.65 us (1%)
    pallas_call x1, Pallas kernels, shards(): pl.pallas_call(functools.partial(kernel, size), out_shape=(jax.ShapeDtype...  58.2 us
    unnamed x8, local copies, waits for them, and re-layouts  4.17 us

profile of v1, /device:TPU:7, one launch (start us, length us, event | category | flops | bytes accessed | tf_op | source)
XLA Modules:
  0.0 63.0 jit_solution(18120408971970136165)
XLA Ops:
  0.6 58.2 %block_sparse_ffn.1 = (bf16[8,1024]{1,0:T(8,128)(2,1)}, bf16[8,1024]{1,0:T(8,128)(2,1)}, f32[8,16,128]{2,1,0:T(8,128)}, f32[8,16,128]{2,1,0:T(8,128)}) custom-call(s32[8]{0:T(128)} %bitcast.12, s32[8]{0:T(128)} %bitcast.13, s32[8]{0:T(128)} %bitcast.14, s32[8]{0:T(128)} %bitcast.15, bf16[128,1024]{1,0:T(8,128)(2,1)} %tok_hbm.1, ...), custom_call_target="tpu_custom_call" | custom-call | tf_op jit(solution)/shard_map/block_sparse_ffn/pallas_call | solution.py:220
  58.8 0.0 copy-start.1
  58.9 1.4 %copy.16 = bf16[8,1024]{1,0:T(8,128)(2,1)} copy(bf16[8,1024]{1,0:T(8,128)(2,1)} %get-tuple-element.16) | data formatting | bytes 32768
  60.2 1.3 %copy.17 = bf16[8,1024]{1,0:T(8,128)(2,1)} copy(bf16[8,1024]{1,0:T(8,128)(2,1)} %get-tuple-element.17) | data formatting | bytes 32768
  61.5 0.0 copy-done.1
  61.5 0.0 copy-start
  61.5 0.6 copy.18
  62.2 0.2 copy-done
  62.4 0.6 copy.19
Async XLA Ops:
  58.8 2.7 %copy-start.1 = (f32[8,16,128]{2,1,0:T(8,128)S(1)}, f32[8,16,128]{2,1,0:T(8,128)}, u32[]{:S(2)}) copy-start(f32[8,16,128]{2,1,0:T(8,128)} %get-tuple-element.10) | copy-start | bytes 196612
  61.5 0.9 %copy-start = (f32[8,16,128]{2,1,0:T(8,128)S(1)}, f32[8,16,128]{2,1,0:T(8,128)}, u32[]{:S(2)}) copy-start(f32[8,16,128]{2,1,0:T(8,128)} %get-tuple-element.11) | copy-start | bytes 196612

commit v2 on v1

v2 whole, which is shorter than its diff:
```python
import functools

import jax
import jax.numpy as jnp
from jax import lax
from jax.experimental import pallas as pl
from jax.experimental.pallas import tpu as pltpu
from jax.sharding import PartitionSpec as P

MESH = pl.DeviceIdType.MESH
F32 = jnp.float32
BF16 = jnp.bfloat16
INV_SQRT2 = 0.7071067811865476
INV_SQRT_2PI = 0.3989422804014327
IDX, IDXC, HID, BACK, ACT, GRAD, OUT, GIN, GW2, GW1 = 0, 1, 2, 3, 4, 6, 8, 10, 12, 14
PHASES = 16


def far_first(size):
    return sorted(range(1, size), key=lambda d: -min(d, size - d))


def kernel(
    size,
    rows1_hbm, cols1_hbm, hid2_hbm, outs2_hbm,
    tok_hbm, w1_hbm, w2_hbm, go_hbm,
    out_hbm, gin_hbm, gw1_hbm, gw2_hbm,
    rows1, cols1, hid2, outs2,
    tok_ref, w1_ref, w2_ref, go_ref,
    out_ref, gin_ref, gw1_ref, gw2_ref,
    key_mine, keys, key_col_mine, keys_col,
    put1, put2, take1, take2, put_rows,
    sh, rh, sb, rb, sa, ra, sg, rg, slope,
    sy1, ry1, sy2, ry2,
    sz1, rz1, sz2, rz2,
    send_sem, recv_sem, in_sem, idx_sem, out_sem,
):
    n_tok, n_row, n_col = size
    row_blocks, tokens, _ = tok_ref.shape
    slots, blk = w1_ref.shape[0], w1_ref.shape[2]
    share = tokens // n_row
    own = tokens // n_col
    half = slots // 2
    t, r, c = lax.axis_index("tok"), lax.axis_index("row"), lax.axis_index("col")

    places = (("row", r, n_row), ("col", c, n_col), ("tok", t, n_tok))
    barrier = pltpu.get_barrier_semaphore()
    for axis, me, count in places:
        for d in far_first(count):
            pl.semaphore_signal(
                barrier, inc=1, device_id={axis: lax.rem(me + d, count)}, device_id_type=MESH
            )

    index_loads = [
        pltpu.make_async_copy(src, dst, idx_sem.at[i])
        for i, (src, dst) in enumerate(
            ((rows1_hbm, rows1), (cols1_hbm, cols1), (hid2_hbm, hid2), (outs2_hbm, outs2))
        )
    ]

    def columns(src, dst, first):
        return [
            pltpu.make_async_copy(src.at[:, b * blk : (b + 1) * blk], dst.at[b], in_sem.at[first + b])
            for b in range(row_blocks)
        ]

    first_loads = columns(tok_hbm, tok_ref, 0)
    first_loads.append(pltpu.make_async_copy(w1_hbm, w1_ref, in_sem.at[2 * row_blocks]))
    second_loads = columns(go_hbm, go_ref, row_blocks)
    second_loads.append(pltpu.make_async_copy(w2_hbm, w2_ref, in_sem.at[2 * row_blocks + 1]))
    for load in index_loads + first_loads + second_loads:
        load.start()

    def copy(src, dst, phase, axis, peer):
        pltpu.make_async_remote_copy(
            src_ref=src,
            dst_ref=dst,
            send_sem=send_sem.at[phase],
            recv_sem=recv_sem.at[phase],
            device_id={axis: peer},
            device_id_type=MESH,
        ).start()

    def wait(span, sem):
        pltpu.make_async_copy(span, span, sem).wait()

    def send_same(axis, me, count, src, dst, phase):
        for d in far_first(count):
            copy(src, dst.at[me], phase, axis, lax.rem(me + d, count))

    def send(axis, me, count, src, dst, phase, lo, n):
        for d in far_first(count):
            peer = lax.rem(me + d, count)
            copy(src.at[peer, pl.ds(lo, n)], dst.at[me, pl.ds(lo, n)], phase, axis, peer)

    def dot(a, b, ca, cb):
        return lax.dot_general(a, b, (((ca,), (cb,)), ((), ())), preferred_element_type=F32)

    for load in index_loads:
        load.wait()

    def key_row(index, first, count, rows, lanes):
        lane = lax.broadcasted_iota(jnp.int32, (1, lanes), 1)
        inner = lax.rem(lane, count * rows)
        key = inner
        for k in range(count):
            inside = (inner >= k * rows) & (inner < (k + 1) * rows)
            key = key + jnp.where(inside, (index[first + k] - k) * rows, 0)
        return key

    lanes, lanes_col = keys.shape[-1], keys_col.shape[-1]
    key_mine[pl.ds(0, 1), :] = key_row(cols1, 0, slots, share, lanes)
    key_mine[pl.ds(1, 1), :] = key_row(hid2, 0, slots, share, lanes)
    for i, (index, first) in enumerate(((outs2, 0), (outs2, half), (rows1, 0), (rows1, half))):
        key_col_mine[pl.ds(i, 1), :] = key_row(index, first, half, own, lanes_col)
    keys[r] = key_mine[...]
    keys_col[c] = key_col_mine[...]

    for load in first_loads:
        load.wait()
    for k in range(slots):
        p = dot(tok_ref[rows1[k]], w1_ref[k], 1, 0)
        sh[:, k] = p.astype(BF16).reshape(n_row, share, blk)
    rh[r] = sh[r]
    pl.semaphore_wait(barrier, n_row + n_col + n_tok - 3)
    send_same("row", r, n_row, key_mine, keys, IDX)
    send("row", r, n_row, sh, rh, HID, 0, slots)
    for load in second_loads:
        load.wait()
    for k in range(slots):
        p = dot(go_ref[outs2[k]], w2_ref[k], 1, 1)
        sb[:, k] = p.astype(BF16).reshape(n_row, share, blk)
    rb[r] = sb[r]
    send("row", r, n_row, sb, rb, BACK, 0, slots)
    send_same("col", c, n_col, key_col_mine, keys_col, IDXC)

    wait(keys.at[pl.ds(0, n_row - 1)], recv_sem.at[IDX])
    held = put1.shape[1]
    held_at = lax.broadcasted_iota(jnp.int32, (held, lanes), 0)

    def build(q, carry):
        for i, (put, take) in enumerate(((put1, take1), (put2, take2))):
            hit = jnp.where(held_at == keys[q, pl.ds(i, 1), :], 1.0, 0.0)
            put[q] = hit.astype(BF16)
            take[q] = hit.T.astype(BF16)
        return carry

    lax.fori_loop(0, n_row, build, 0)

    def place(put, buf):
        total = dot(put[0], buf[0].reshape(slots * share, blk), 1, 0)
        for q in range(1, n_row):
            total += dot(put[q], buf[q].reshape(slots * share, blk), 1, 0)
        return total

    def pick(take, value, dst):
        for q in range(n_row):
            dst[q] = dot(take[q], value, 1, 0).astype(BF16).reshape(slots, share, blk)

    wait(rh.at[pl.ds(0, n_row - 1)], recv_sem.at[HID])
    hidden = place(put1, rh)
    cdf = 0.5 * (1.0 + lax.erf(hidden * INV_SQRT2))
    pick(take2, (hidden * cdf).astype(BF16), sa)
    ra[r] = sa[r]
    send("row", r, n_row, sa, ra, ACT, 0, half)
    send("row", r, n_row, sa, ra, ACT + 1, half, half)
    slope[...] = cdf + hidden * jnp.exp(-0.5 * hidden * hidden) * INV_SQRT_2PI

    wait(keys_col.at[pl.ds(0, n_col - 1)], recv_sem.at[IDXC])
    group = lanes_col // (half * own)
    rows_at = lax.broadcasted_iota(jnp.int32, (row_blocks * own, lanes_col), 0)
    lane = lax.broadcasted_iota(jnp.int32, (1, lanes_col), 1)
    for i in range(4):
        for g in range(n_col // group):
            key = keys_col[g * group, pl.ds(i, 1), :]
            for j in range(1, group):
                key = jnp.where(lane >= j * half * own, keys_col[g * group + j, pl.ds(i, 1), :], key)
            hit = jnp.where(rows_at == key, 1.0, 0.0)
            put_rows[i, :, g * lanes_col : (g + 1) * lanes_col] = hit.astype(BF16)

    wait(rb.at[pl.ds(0, n_row - 1)], recv_sem.at[BACK])
    pick(take1, (place(put2, rb) * slope[...]).astype(BF16), sg)
    rg[r] = sg[r]
    send("row", r, n_row, sg, rg, GRAD, 0, half)
    send("row", r, n_row, sg, rg, GRAD + 1, half, half)

    def rows_out(got, weights, cb, dst, recv, phase, lo):
        for j in range(lo // 2, (lo + half) // 2):
            pair = [
                dot(got[:, k].reshape(tokens, blk), weights[k], 1, cb).reshape(n_col, own, blk)
                for k in (2 * j, 2 * j + 1)
            ]
            dst[:, j] = jnp.concatenate(pair, axis=1).astype(BF16)
        recv[c, pl.ds(lo // 2, half // 2)] = dst[c, pl.ds(lo // 2, half // 2)]
        send("col", c, n_col, dst, recv, phase, lo // 2, half // 2)

    def strips_out(lefts, rights, dst, recv, phase, lo):
        for k in range(lo, lo + half):
            p = dot(lefts(k), rights(k), 0, 0)
            dst[:, k] = p.astype(BF16).reshape(n_tok, blk // n_tok, blk)
        recv[t, pl.ds(lo, half)] = dst[t, pl.ds(lo, half)]
        send("tok", t, n_tok, dst, recv, phase, lo, half)

    def arrived(buf, count, phase, lo, n):
        wait(buf.at[pl.ds(0, count - 1), pl.ds(lo, n)], recv_sem.at[phase])

    def placed_rows(buf, part, which):
        got = buf[:, part * half // 2 : (part + 1) * half // 2].reshape(n_col * half * own, blk)
        return dot(put_rows[which + part], got, 1, 0)

    def write_rows(total, out, out_to, i):
        for b in range(row_blocks):
            out[:, b * blk : (b + 1) * blk] = total[b * own : (b + 1) * own].astype(BF16)
        write = pltpu.make_async_copy(out, out_to, out_sem.at[i])
        write.start()
        return write

    def act_part(part):
        lo = part * half
        arrived(ra, n_row, ACT + part, lo, half)
        rows_out(ra, w2_ref, 0, sy1, ry1, OUT + part, lo)
        strips_out(
            lambda k: ra[:, k].reshape(tokens, blk), lambda k: go_ref[outs2[k]], sz2, rz2, GW2 + part, lo
        )

    def grad_part(part):
        lo = part * half
        arrived(rg, n_row, GRAD + part, lo, half)
        rows_out(rg, w1_ref, 1, sy2, ry2, GIN + part, lo)
        strips_out(
            lambda k: tok_ref[rows1[k]], lambda k: rg[:, k].reshape(tokens, blk), sz1, rz1, GW1 + part, lo
        )

    act_part(0)
    act_part(1)
    grad_part(0)
    for part in range(2):
        arrived(ry1, n_col, OUT + part, part * half // 2, half // 2)
    writes = [write_rows(placed_rows(ry1, 0, 0) + placed_rows(ry1, 1, 0), out_ref, out_hbm, 0)]
    grad_part(1)

    def strips_in(buf, part, phase, out):
        lo = part * half
        arrived(buf, n_tok, phase + part, lo, half)
        out[pl.ds(lo, half)] = jnp.sum(buf[:, lo : lo + half].astype(F32), axis=0)

    def write_strips(out, out_to, i):
        writes.append(pltpu.make_async_copy(out, out_to, out_sem.at[i]))
        writes[-1].start()

    strips_in(rz2, 0, GW2, gw2_ref)
    strips_in(rz2, 1, GW2, gw2_ref)
    write_strips(gw2_ref, gw2_hbm, 3)
    strips_in(rz1, 0, GW1, gw1_ref)
    arrived(ry2, n_col, GIN, 0, half // 2)
    first_rows = placed_rows(ry2, 0, 2)
    strips_in(rz1, 1, GW1, gw1_ref)
    write_strips(gw1_ref, gw1_hbm, 2)
    arrived(ry2, n_col, GIN + 1, half // 2, half // 2)
    writes.append(write_rows(first_rows + placed_rows(ry2, 1, 2), gin_ref, gin_hbm, 1))

    wait(keys.at[pl.ds(0, n_row - 1)], send_sem.at[IDX])
    wait(keys_col.at[pl.ds(0, n_col - 1)], send_sem.at[IDXC])
    wait(sh.at[pl.ds(0, n_row - 1)], send_sem.at[HID])
    wait(sb.at[pl.ds(0, n_row - 1)], send_sem.at[BACK])
    for part in range(2):
        lo = part * half
        for buf, count, phase, at, n in (
            (sa, n_row, ACT, lo, half), (sg, n_row, GRAD, lo, half),
            (sy1, n_col, OUT, lo // 2, half // 2), (sy2, n_col, GIN, lo // 2, half // 2),
            (sz2, n_tok, GW2, lo, half), (sz1, n_tok, GW1, lo, half),
        ):
            wait(buf.at[pl.ds(0, count - 1), pl.ds(at, n)], send_sem.at[phase + part])
    for write in writes:
        write.wait()


def write_results(*refs):
    for src, dst in zip(refs[:4], refs[4:]):
        dst[...] = src[...]


def shards(size, hidden_width, tokens, w1_blocks, w1_rows, w1_cols, w2_blocks, w2_hidden, w2_outs, grad_out):
    n_tok, n_row, n_col = size
    slots, blk = w1_blocks.shape[2], w1_blocks.shape[-1]
    rows, width = tokens.shape
    col_blocks = hidden_width // n_col // blk
    share, own, strip = rows // n_row, rows // n_col, blk // n_tok
    any_spec = pl.BlockSpec(memory_space=pl.ANY)
    vmem = pl.BlockSpec(memory_space=pltpu.VMEM)
    held = col_blocks * share
    lanes, lanes_col = slots * share, max(blk, slots // 2 * own)
    along_row = pltpu.VMEM((n_row, slots, share, blk), BF16)
    along_col = pltpu.VMEM((n_col, slots // 2, 2 * own, blk), BF16)
    along_tok = pltpu.VMEM((n_tok, slots, strip, blk), BF16)
    shapes = (
        jax.ShapeDtypeStruct((own, width), BF16),
        jax.ShapeDtypeStruct((own, width), BF16),
        jax.ShapeDtypeStruct((slots, strip, blk), F32),
        jax.ShapeDtypeStruct((slots, strip, blk), F32),
    )
    results = pl.pallas_call(
        functools.partial(kernel, size),
        out_shape=shapes,
        in_specs=[any_spec] * 8,
        out_specs=[any_spec] * 4,
        scratch_shapes=[pltpu.SMEM((slots,), jnp.int32)] * 4
        + [
            pltpu.VMEM((width // blk, rows, blk), BF16),
            pltpu.VMEM((slots, blk, blk), BF16),
            pltpu.VMEM((slots, blk, blk), BF16),
            pltpu.VMEM((width // blk, rows, blk), BF16),
        ]
        + [pltpu.VMEM(shape.shape, shape.dtype) for shape in shapes]
        + [
            pltpu.VMEM((2, lanes), jnp.int32),
            pltpu.VMEM((n_row, 2, lanes), jnp.int32),
            pltpu.VMEM((4, lanes_col), jnp.int32),
            pltpu.VMEM((n_col, 4, lanes_col), jnp.int32),
            pltpu.VMEM((n_row, held, lanes), BF16),
            pltpu.VMEM((n_row, held, lanes), BF16),
            pltpu.VMEM((n_row, lanes, held), BF16),
            pltpu.VMEM((n_row, lanes, held), BF16),
            pltpu.VMEM((4, width // blk * own, n_col * slots // 2 * own), BF16),
        ]
        + [along_row] * 8
        + [pltpu.VMEM((held, blk), F32)]
        + [along_col] * 4
        + [along_tok] * 4
        + [
            pltpu.SemaphoreType.DMA((PHASES,)),
            pltpu.SemaphoreType.DMA((PHASES,)),
            pltpu.SemaphoreType.DMA((2 * (width // blk) + 2,)),
            pltpu.SemaphoreType.DMA((4,)),
            pltpu.SemaphoreType.DMA((4,)),
        ],
        compiler_params=pltpu.CompilerParams(collective_id=0, has_side_effects=True),
        name="block_sparse_ffn",
    )(
        w1_rows.reshape(slots), w1_cols.reshape(slots), w2_hidden.reshape(slots), w2_outs.reshape(slots),
        tokens, w1_blocks.reshape(slots, blk, blk), w2_blocks.reshape(slots, blk, blk), grad_out,
    )
    out, gin, gw1, gw2 = pl.pallas_call(
        write_results, out_shape=shapes, in_specs=[vmem] * 4, out_specs=[vmem] * 4, name="write_results"
    )(*results)
    return out, gin, gw1.reshape(1, 1, slots, strip, blk), gw2.reshape(1, 1, slots, strip, blk)


def solution(mesh, hidden_width=32768):
    placed = (
        P("tok", "row"),
        P("row", "col", None, None, None),
        P("row", "col", None),
        P("row", "col", None),
        P("row", "col", None, None, None),
        P("row", "col", None),
        P("row", "col", None),
        P("tok", "row"),
    )
    size = tuple(mesh.shape[axis] for axis in ("tok", "row", "col"))
    return jax.shard_map(
        functools.partial(shards, size, hidden_width),
        mesh=mesh,
        in_specs=placed,
        out_specs=(
            P(("tok", "col"), "row"),
            P(("tok", "col"), "row"),
            P("row", "col", None, "tok", None),
            P("row", "col", None, "tok", None),
        ),
        check_vma=False,
    )
```

time: 63.3 us -> 58.4 us (0.923)
  the two profiles are of different devices: /device:TPU:7 before, /device:TPU:1 now
where the time goes in v2:
time: 58.4 us; the launch traced here: 58.1 us
  Pallas kernels  57.5 us (98%)
  between operations  0.64 us (1%)
    pallas_call x1, Pallas kernels, shards(): pl.pallas_call(functools.partial(kernel, size), out_shape=shapes, in_spec...  55.9 us
    pallas_call x1, Pallas kernels, shards(): pl.pallas_call(write_results, out_shape=shapes, in_specs=[vmem] * 4, out_...  1.57 us

profile of v2, /device:TPU:1, one launch (start us, length us, event | category | flops | bytes accessed | tf_op | source)
XLA Modules:
  0.0 58.1 jit_solution(9152641937135591284)
XLA Ops:
  0.6 55.9 %block_sparse_ffn.1 = (bf16[8,1024]{1,0:T(8,128)(2,1)}, bf16[8,1024]{1,0:T(8,128)(2,1)}, f32[8,16,128]{2,1,0:T(8,128)}, f32[8,16,128]{2,1,0:T(8,128)}) custom-call(s32[8]{0:T(128)} %bitcast.10, s32[8]{0:T(128)} %bitcast.11, s32[8]{0:T(128)} %bitcast.12, s32[8]{0:T(128)} %bitcast.13, bf16[128,1024]{1,0:T(8,128)(2,1)} %tok_hbm.1, ...), custom_call_target="tpu_custom_call" | custom-call | tf_op jit(solution)/shard_map/block_sparse_ffn/pallas_call | solution.py:302
  56.6 1.6 %write_results.1 = (bf16[8,1024]{1,0:T(8,128)(2,1)}, bf16[8,1024]{1,0:T(8,128)(2,1)}, f32[8,16,128]{2,1,0:T(8,128)}, f32[8,16,128]{2,1,0:T(8,128)}) custom-call(bf16[8,1024]{1,0:T(8,128)(2,1)} %get-tuple-element.12.refs_0_, bf16[8,1024]{1,0:T(8,128)(2,1)} %get-tuple-element.13.refs_1_, f32[8,16,128]{2,1,0:T(8,128)} %get-tuple-element.14.refs_2_, ...), custom_call_target="tpu_custom_call" | custom-call | tf_op jit(solution)/shard_map/write_results/pallas_call | solution.py:343

commit v3 on v2

v3 whole, which is shorter than its diff:
```python
import functools

import jax
import jax.numpy as jnp
from jax import lax
from jax.experimental import pallas as pl
from jax.experimental.pallas import tpu as pltpu
from jax.sharding import PartitionSpec as P

MESH = pl.DeviceIdType.MESH
F32 = jnp.float32
BF16 = jnp.bfloat16
INV_SQRT2 = 0.7071067811865476
INV_SQRT_2PI = 0.3989422804014327
IDX, IDXC, HID, BACK, ACT, OUT, GW2, GRAD, GIN, GW1 = 0, 1, 2, 3, 4, 8, 12, 16, 20, 24
PHASES = 28


def cut(slots):
    q = slots // 4
    return ((0, 2 * q), (2 * q, 2 * q)), ((0, 2 * q), (2 * q, 2 * q))


def far_first(size):
    return sorted(range(1, size), key=lambda d: -min(d, size - d))


def kernel(
    size,
    rows1_hbm, cols1_hbm, hid2_hbm, outs2_hbm,
    tok_hbm, w1_hbm, w2_hbm, go_hbm,
    out_ref, gin_ref, gw1_ref, gw2_ref,
    rows1, cols1, hid2, outs2,
    tok_ref, w1_ref, w2_ref, go_ref,
    key_mine, keys, key_col_mine, keys_col,
    put1, put2, take1, take2,
    sh, rh, sb, rb, sa, ra, sg, rg, slope,
    sy1, ry1, sy2, ry2,
    sz1, rz1, sz2, rz2,
    send_sem, recv_sem, in_sem, idx_sem, *put_rows,
):
    n_tok, n_row, n_col = size
    row_blocks, tokens, _ = tok_ref.shape
    slots, blk = w1_ref.shape[0], w1_ref.shape[2]
    share = tokens // n_row
    own = tokens // n_col
    act_parts, grad_parts = cut(slots)
    t, r, c = lax.axis_index("tok"), lax.axis_index("row"), lax.axis_index("col")

    index_loads = [
        pltpu.make_async_copy(src, dst, idx_sem.at[i])
        for i, (src, dst) in enumerate(
            ((rows1_hbm, rows1), (cols1_hbm, cols1), (hid2_hbm, hid2), (outs2_hbm, outs2))
        )
    ]

    def columns(src, dst, first):
        return [
            pltpu.make_async_copy(src.at[:, b * blk : (b + 1) * blk], dst.at[b], in_sem.at[first + b])
            for b in range(row_blocks)
        ]

    first_loads = columns(tok_hbm, tok_ref, 0)
    first_loads.append(pltpu.make_async_copy(w1_hbm, w1_ref, in_sem.at[2 * row_blocks]))
    second_loads = columns(go_hbm, go_ref, row_blocks)
    second_loads.append(pltpu.make_async_copy(w2_hbm, w2_ref, in_sem.at[2 * row_blocks + 1]))
    for load in index_loads + first_loads + second_loads:
        load.start()

    places = (("row", r, n_row), ("col", c, n_col), ("tok", t, n_tok))
    barrier = pltpu.get_barrier_semaphore()
    for axis, me, count in places:
        for d in far_first(count):
            pl.semaphore_signal(
                barrier, inc=1, device_id={axis: lax.rem(me + d, count)}, device_id_type=MESH
            )

    def copy(src, dst, phase, axis, peer):
        pltpu.make_async_remote_copy(
            src_ref=src,
            dst_ref=dst,
            send_sem=send_sem.at[phase],
            recv_sem=recv_sem.at[phase],
            device_id={axis: peer},
            device_id_type=MESH,
        ).start()

    def wait(span, sem):
        pltpu.make_async_copy(span, span, sem).wait()

    def send_same(axis, me, count, src, dst, phase):
        for d in far_first(count):
            copy(src, dst.at[me], phase, axis, lax.rem(me + d, count))

    def send(axis, me, count, src, dst, phase, lo, n):
        for d in far_first(count):
            peer = lax.rem(me + d, count)
            copy(src.at[peer, pl.ds(lo, n)], dst.at[me, pl.ds(lo, n)], phase, axis, peer)

    def dot(a, b, ca, cb):
        return lax.dot_general(a, b, (((ca,), (cb,)), ((), ())), preferred_element_type=F32)

    for load in index_loads:
        load.wait()

    def key_row(index, first, count, rows, lanes):
        lane = lax.broadcasted_iota(jnp.int32, (1, lanes), 1)
        inner = lax.rem(lane, count * rows)
        key = inner
        for k in range(count):
            inside = (inner >= k * rows) & (inner < (k + 1) * rows)
            key = key + jnp.where(inside, (index[first + k] - k) * rows, 0)
        return key

    lanes, lanes_col = keys.shape[-1], keys_col.shape[-1]
    key_mine[pl.ds(0, 1), :] = key_row(cols1, 0, slots, share, lanes)
    key_mine[pl.ds(1, 1), :] = key_row(hid2, 0, slots, share, lanes)
    row_parts = [(outs2, *part) for part in act_parts] + [(rows1, *part) for part in grad_parts]
    for i, (index, lo, n) in enumerate(row_parts):
        key_col_mine[pl.ds(i, 1), :] = key_row(index, lo, n, own, lanes_col)
    keys[r] = key_mine[...]
    keys_col[c] = key_col_mine[...]

    for load in first_loads:
        load.wait()
    for k in range(slots):
        p = dot(tok_ref[rows1[k]], w1_ref[k], 1, 0)
        sh[:, k] = p.astype(BF16).reshape(n_row, share, blk)
    rh[r] = sh[r]
    pl.semaphore_wait(barrier, n_row + n_col + n_tok - 3)
    send_same("row", r, n_row, key_mine, keys, IDX)
    send("row", r, n_row, sh, rh, HID, 0, slots)
    for load in second_loads:
        load.wait()
    for k in range(slots):
        p = dot(go_ref[outs2[k]], w2_ref[k], 1, 1)
        sb[:, k] = p.astype(BF16).reshape(n_row, share, blk)
    rb[r] = sb[r]
    send("row", r, n_row, sb, rb, BACK, 0, slots)
    send_same("col", c, n_col, key_col_mine, keys_col, IDXC)

    wait(keys.at[pl.ds(0, n_row - 1)], recv_sem.at[IDX])
    held = put1.shape[1]
    held_at = lax.broadcasted_iota(jnp.int32, (held, lanes), 0)

    def build(q, carry):
        for i, (put, take) in enumerate(((put1, take1), (put2, take2))):
            hit = jnp.where(held_at == keys[q, pl.ds(i, 1), :], 1.0, 0.0)
            put[q] = hit.astype(BF16)
            take[q] = hit.T.astype(BF16)
        return carry

    lax.fori_loop(0, n_row, build, 0)

    def place(put, buf):
        total = dot(put[0], buf[0].reshape(slots * share, blk), 1, 0)
        for q in range(1, n_row):
            total += dot(put[q], buf[q].reshape(slots * share, blk), 1, 0)
        return total

    def pick(take, value, dst, got, phase, parts):
        for i, (lo, n) in enumerate(parts):
            for q in range(n_row):
                rows = take[q, lo * share : (lo + n) * share]
                dst[q, pl.ds(lo, n)] = dot(rows, value, 1, 0).astype(BF16).reshape(n, share, blk)
            send("row", r, n_row, dst, got, phase + i, lo, n)
        got[r] = dst[r]

    wait(rh.at[pl.ds(0, n_row - 1)], recv_sem.at[HID])
    hidden = place(put1, rh)
    cdf = 0.5 * (1.0 + lax.erf(hidden * INV_SQRT2))
    pick(take2, (hidden * cdf).astype(BF16), sa, ra, ACT, act_parts)
    slope[...] = cdf + hidden * jnp.exp(-0.5 * hidden * hidden) * INV_SQRT_2PI

    wait(keys_col.at[pl.ds(0, n_col - 1)], recv_sem.at[IDXC])
    rows_at = lax.broadcasted_iota(jnp.int32, (row_blocks * own, lanes_col), 0)
    lane = lax.broadcasted_iota(jnp.int32, (1, lanes_col), 1)
    for i, (_, _, n) in enumerate(row_parts):
        group = lanes_col // (n * own)
        for g in range(n_col // group):
            key = keys_col[g * group, pl.ds(i, 1), :]
            for j in range(1, group):
                key = jnp.where(lane >= j * n * own, keys_col[g * group + j, pl.ds(i, 1), :], key)
            hit = jnp.where(rows_at == key, 1.0, 0.0)
            put_rows[i][:, g * lanes_col : (g + 1) * lanes_col] = hit.astype(BF16)

    wait(rb.at[pl.ds(0, n_row - 1)], recv_sem.at[BACK])
    pick(take1, (place(put2, rb) * slope[...]).astype(BF16), sg, rg, GRAD, grad_parts)

    def rows_out(got, weights, cb, dst, recv, phase, lo, n):
        for j in range(lo // 2, (lo + n) // 2):
            pair = [
                dot(got[:, k].reshape(tokens, blk), weights[k], 1, cb).reshape(n_col, own, blk)
                for k in (2 * j, 2 * j + 1)
            ]
            dst[:, j] = jnp.concatenate(pair, axis=1).astype(BF16)
        recv[c, pl.ds(lo // 2, n // 2)] = dst[c, pl.ds(lo // 2, n // 2)]
        send("col", c, n_col, dst, recv, phase, lo // 2, n // 2)

    def strips_out(lefts, rights, dst, recv, phase, lo, n):
        for k in range(lo, lo + n):
            p = dot(lefts(k), rights(k), 0, 0)
            dst[:, k] = p.astype(BF16).reshape(n_tok, blk // n_tok, blk)
        recv[t, pl.ds(lo, n)] = dst[t, pl.ds(lo, n)]
        send("tok", t, n_tok, dst, recv, phase, lo, n)

    def arrived(buf, count, phase, lo, n):
        wait(buf.at[pl.ds(0, count - 1), pl.ds(lo, n)], recv_sem.at[phase])

    def rows_in(buf, phase, i, lo, n, put):
        arrived(buf, n_col, phase + i, lo // 2, n // 2)
        got = buf[:, lo // 2 : (lo + n) // 2].reshape(n_col * n * own, blk)
        return dot(put[...], got, 1, 0)

    def write_rows(total, out):
        for b in range(row_blocks):
            out[:, b * blk : (b + 1) * blk] = total[b * own : (b + 1) * own].astype(BF16)

    def strips_in(buf, phase, i, lo, n, out):
        arrived(buf, n_tok, phase + i, lo, n)
        out[pl.ds(lo, n)] = jnp.sum(buf[:, lo : lo + n].astype(F32), axis=0)

    def block(ref):
        return lambda k: ref[:, k].reshape(tokens, blk)

    def act_part(i):
        lo, n = act_parts[i]
        arrived(ra, n_row, ACT + i, lo, n)
        rows_out(ra, w2_ref, 0, sy1, ry1, OUT + i, lo, n)
        strips_out(block(ra), lambda k: go_ref[outs2[k]], sz2, rz2, GW2 + i, lo, n)

    def grad_part(i):
        lo, n = grad_parts[i]
        arrived(rg, n_row, GRAD + i, lo, n)
        rows_out(rg, w1_ref, 1, sy2, ry2, GIN + i, lo, n)
        strips_out(lambda k: tok_ref[rows1[k]], block(rg), sz1, rz1, GW1 + i, lo, n)

    puts_out, puts_gin = put_rows[: len(act_parts)], put_rows[len(act_parts) :]
    for i in range(len(act_parts)):
        act_part(i)
    if len(grad_parts) > 1:
        grad_part(0)
    rows = [rows_in(ry1, OUT, i, *part, puts_out[i]) for i, part in enumerate(act_parts)]
    write_rows(functools.reduce(jnp.add, rows), out_ref)
    for i in range(1 if len(grad_parts) > 1 else 0, len(grad_parts)):
        grad_part(i)
    rows = rows_in(ry2, GIN, 0, *grad_parts[0], puts_gin[0])
    for i, part in enumerate(act_parts):
        strips_in(rz2, GW2, i, *part, gw2_ref)
    strips_in(rz1, GW1, 0, *grad_parts[0], gw1_ref)
    for i in range(1, len(grad_parts)):
        rows += rows_in(ry2, GIN, i, *grad_parts[i], puts_gin[i])
        strips_in(rz1, GW1, i, *grad_parts[i], gw1_ref)
    write_rows(rows, gin_ref)

    wait(keys.at[pl.ds(0, n_row - 1)], send_sem.at[IDX])
    wait(keys_col.at[pl.ds(0, n_col - 1)], send_sem.at[IDXC])
    wait(sh.at[pl.ds(0, n_row - 1)], send_sem.at[HID])
    wait(sb.at[pl.ds(0, n_row - 1)], send_sem.at[BACK])
    for parts, along in (
        (act_parts, ((sa, n_row, ACT, 1), (sy1, n_col, OUT, 2), (sz2, n_tok, GW2, 1))),
        (grad_parts, ((sg, n_row, GRAD, 1), (sy2, n_col, GIN, 2), (sz1, n_tok, GW1, 1))),
    ):
        for buf, count, phase, per in along:
            for i, (lo, n) in enumerate(parts):
                wait(buf.at[pl.ds(0, count - 1), pl.ds(lo // per, n // per)], send_sem.at[phase + i])


def write_results(*refs):
    sources, targets, sem = refs[:4], refs[4:8], refs[8]
    writes = [pltpu.make_async_copy(s, d, sem.at[i]) for i, (s, d) in enumerate(zip(sources, targets))]
    for write in writes:
        write.start()
    for write in writes:
        write.wait()


def shards(size, hidden_width, tokens, w1_blocks, w1_rows, w1_cols, w2_blocks, w2_hidden, w2_outs, grad_out):
    n_tok, n_row, n_col = size
    slots, blk = w1_blocks.shape[2], w1_blocks.shape[-1]
    rows, width = tokens.shape
    col_blocks = hidden_width // n_col // blk
    share, own, strip = rows // n_row, rows // n_col, blk // n_tok
    any_spec = pl.BlockSpec(memory_space=pl.ANY)
    vmem = pl.BlockSpec(memory_space=pltpu.VMEM)
    held = col_blocks * share
    act_parts, grad_parts = cut(slots)
    parts = act_parts + grad_parts
    lanes, lanes_col = slots * share, max(blk, slots // 2 * own)
    along_row = pltpu.VMEM((n_row, slots, share, blk), BF16)
    along_col = pltpu.VMEM((n_col, slots // 2, 2 * own, blk), BF16)
    along_tok = pltpu.VMEM((n_tok, slots, strip, blk), BF16)
    shapes = (
        jax.ShapeDtypeStruct((own, width), BF16),
        jax.ShapeDtypeStruct((own, width), BF16),
        jax.ShapeDtypeStruct((slots, strip, blk), F32),
        jax.ShapeDtypeStruct((slots, strip, blk), F32),
    )
    results = pl.pallas_call(
        functools.partial(kernel, size),
        out_shape=tuple(pltpu.VMEM(shape.shape, shape.dtype) for shape in shapes),
        in_specs=[any_spec] * 8,
        out_specs=[vmem] * 4,
        scratch_shapes=[pltpu.SMEM((slots,), jnp.int32)] * 4
        + [
            pltpu.VMEM((width // blk, rows, blk), BF16),
            pltpu.VMEM((slots, blk, blk), BF16),
            pltpu.VMEM((slots, blk, blk), BF16),
            pltpu.VMEM((width // blk, rows, blk), BF16),
        ]
        + [
            pltpu.VMEM((2, lanes), jnp.int32),
            pltpu.VMEM((n_row, 2, lanes), jnp.int32),
            pltpu.VMEM((len(parts), lanes_col), jnp.int32),
            pltpu.VMEM((n_col, len(parts), lanes_col), jnp.int32),
            pltpu.VMEM((n_row, held, lanes), BF16),
            pltpu.VMEM((n_row, held, lanes), BF16),
            pltpu.VMEM((n_row, lanes, held), BF16),
            pltpu.VMEM((n_row, lanes, held), BF16),
        ]
        + [along_row] * 8
        + [pltpu.VMEM((held, blk), F32)]
        + [along_col] * 4
        + [along_tok] * 4
        + [
            pltpu.SemaphoreType.DMA((PHASES,)),
            pltpu.SemaphoreType.DMA((PHASES,)),
            pltpu.SemaphoreType.DMA((2 * (width // blk) + 2,)),
            pltpu.SemaphoreType.DMA((4,)),
        ]
        + [pltpu.VMEM((width // blk * own, n_col * n * own), BF16) for _, n in parts],
        compiler_params=pltpu.CompilerParams(collective_id=0, has_side_effects=True),
        name="block_sparse_ffn",
    )(
        w1_rows.reshape(slots), w1_cols.reshape(slots), w2_hidden.reshape(slots), w2_outs.reshape(slots),
        tokens, w1_blocks.reshape(slots, blk, blk), w2_blocks.reshape(slots, blk, blk), grad_out,
    )
    out, gin, gw1, gw2 = pl.pallas_call(
        write_results,
        out_shape=shapes,
        in_specs=[vmem] * 4,
        out_specs=[any_spec] * 4,
        scratch_shapes=[pltpu.SemaphoreType.DMA((4,))],
        name="write_results",
    )(*(pltpu.with_memory_space_constraint(held, pltpu.VMEM) for held in results))
    return out, gin, gw1.reshape(1, 1, slots, strip, blk), gw2.reshape(1, 1, slots, strip, blk)


def solution(mesh, hidden_width=32768):
    placed = (
        P("tok", "row"),
        P("row", "col", None, None, None),
        P("row", "col", None),
        P("row", "col", None),
        P("row", "col", None, None, None),
        P("row", "col", None),
        P("row", "col", None),
        P("tok", "row"),
    )
    size = tuple(mesh.shape[axis] for axis in ("tok", "row", "col"))
    return jax.shard_map(
        functools.partial(shards, size, hidden_width),
        mesh=mesh,
        in_specs=placed,
        out_specs=(
            P(("tok", "col"), "row"),
            P(("tok", "col"), "row"),
            P("row", "col", None, "tok", None),
            P("row", "col", None, "tok", None),
        ),
        check_vma=False,
    )
```

time: 58.4 us -> 56.8 us (0.973)
  Pallas kernels: 57.5 us -> 56 us
    pallas_call x1, Pallas kernels: 1.57 us -> 0.7 us  [shards(): pl.pallas_call(write_results, out_shape=shapes, in_specs=[vmem] * 4, out_...]
    pallas_call x1, Pallas kernels: 55.9 us -> 55.3 us  [shards(): pl.pallas_call(functools.partial(kernel, size), out_shape=tuple((pltpu.VM...]
where the time goes in v3:
time: 56.8 us; the launch traced here: 56.6 us
  Pallas kernels  56 us (99%)
  between operations  0.64 us (1%)
    pallas_call x1, Pallas kernels, shards(): pl.pallas_call(functools.partial(kernel, size), out_shape=tuple((pltpu.VM...  55.3 us

profile of v3, /device:TPU:1, one launch (start us, length us, event | category | flops | bytes accessed | tf_op | source)
XLA Modules:
  0.0 56.6 jit_solution(1059111144333110623)
XLA Ops:
  0.6 55.3 %block_sparse_ffn.1 = (bf16[8,1024]{1,0:T(8,128)(2,1)S(1)}, bf16[8,1024]{1,0:T(8,128)(2,1)S(1)}, f32[8,16,128]{2,1,0:T(8,128)S(1)}, f32[8,16,128]{2,1,0:T(8,128)S(1)}) custom-call(s32[8]{0:T(128)} %bitcast.10, s32[8]{0:T(128)} %bitcast.11, s32[8]{0:T(128)} %bitcast.12, s32[8]{0:T(128)} %bitcast.13, bf16[128,1024]{1,0:T(8,128)(2,1)} %tok_hbm.1, ...), custom_call_target="tpu_custom_call" | custom-call | tf_op jit(solution)/shard_map/block_sparse_ffn/pallas_call | solution.py:299
  55.9 0.7 %write_results.1 = (bf16[8,1024]{1,0:T(8,128)(2,1)}, bf16[8,1024]{1,0:T(8,128)(2,1)}, f32[8,16,128]{2,1,0:T(8,128)}, f32[8,16,128]{2,1,0:T(8,128)}) custom-call(bf16[8,1024]{1,0:T(8,128)(2,1)S(1)} %get-tuple-element.12.refs_0_, bf16[8,1024]{1,0:T(8,128)(2,1)S(1)} %get-tuple-element.13.refs_1_, f32[8,16,128]{2,1,0:T(8,128)S(1)} %get-tuple-element.14.refs_2_, ...), custom_call_target="tpu_custom_call" | custom-call | tf_op jit(solution)/shard_map/write_results/pallas_call | solution.py:338

commit v4 on v3

--- a/solution.py
+++ b/solution.py
@@ -240,10 +240,10 @@
         act_part(i)
     if len(grad_parts) > 1:
         grad_part(0)
+    for i in range(1 if len(grad_parts) > 1 else 0, len(grad_parts)):
+        grad_part(i)
     rows = [rows_in(ry1, OUT, i, *part, puts_out[i]) for i, part in enumerate(act_parts)]
     write_rows(functools.reduce(jnp.add, rows), out_ref)
-    for i in range(1 if len(grad_parts) > 1 else 0, len(grad_parts)):
-        grad_part(i)
     rows = rows_in(ry2, GIN, 0, *grad_parts[0], puts_gin[0])
     for i, part in enumerate(act_parts):
         strips_in(rz2, GW2, i, *part, gw2_ref)

time: 56.8 us -> 56.2 us (0.989)
  Pallas kernels: 56 us -> 55.4 us
where the time goes in v4:
time: 56.2 us; the launch traced here: 56 us
  Pallas kernels  55.4 us (99%)
  between operations  0.64 us (1%)
    pallas_call x1, Pallas kernels, shards(): pl.pallas_call(functools.partial(kernel, size), out_shape=tuple((pltpu.VM...  54.7 us

profile of v4, /device:TPU:1, one launch (start us, length us, event | category | flops | bytes accessed | tf_op | source)
XLA Modules:
  0.0 56.0 jit_solution(2268753747531203507)
XLA Ops:
  0.6 54.7 %block_sparse_ffn.1 = (bf16[8,1024]{1,0:T(8,128)(2,1)S(1)}, bf16[8,1024]{1,0:T(8,128)(2,1)S(1)}, f32[8,16,128]{2,1,0:T(8,128)S(1)}, f32[8,16,128]{2,1,0:T(8,128)S(1)}) custom-call(s32[8]{0:T(128)} %bitcast.10, s32[8]{0:T(128)} %bitcast.11, s32[8]{0:T(128)} %bitcast.12, s32[8]{0:T(128)} %bitcast.13, bf16[128,1024]{1,0:T(8,128)(2,1)} %tok_hbm.1, ...), custom_call_target="tpu_custom_call" | custom-call | tf_op jit(solution)/shard_map/block_sparse_ffn/pallas_call | solution.py:299
  55.3 0.7 %write_results.1 = (bf16[8,1024]{1,0:T(8,128)(2,1)}, bf16[8,1024]{1,0:T(8,128)(2,1)}, f32[8,16,128]{2,1,0:T(8,128)}, f32[8,16,128]{2,1,0:T(8,128)}) custom-call(bf16[8,1024]{1,0:T(8,128)(2,1)S(1)} %get-tuple-element.12.refs_0_, bf16[8,1024]{1,0:T(8,128)(2,1)S(1)} %get-tuple-element.13.refs_1_, f32[8,16,128]{2,1,0:T(8,128)S(1)} %get-tuple-element.14.refs_2_, ...), custom_call_target="tpu_custom_call" | custom-call | tf_op jit(solution)/shard_map/write_results/pallas_call | solution.py:338

commit v5 on v4

--- a/solution.py
+++ b/solution.py
@@ -250,8 +250,9 @@
     strips_in(rz1, GW1, 0, *grad_parts[0], gw1_ref)
     for i in range(1, len(grad_parts)):
         rows += rows_in(ry2, GIN, i, *grad_parts[i], puts_gin[i])
+        if i == len(grad_parts) - 1:
+            write_rows(rows, gin_ref)
         strips_in(rz1, GW1, i, *grad_parts[i], gw1_ref)
-    write_rows(rows, gin_ref)
 
     wait(keys.at[pl.ds(0, n_row - 1)], send_sem.at[IDX])
     wait(keys_col.at[pl.ds(0, n_col - 1)], send_sem.at[IDXC])

time: 56.2 us -> 56.2 us (level)
  no operation moved by 1% of the time
where the time goes in v5:
time: 56.2 us; the launch traced here: 56.1 us
  Pallas kernels  55.4 us (99%)
  between operations  0.64 us (1%)
    pallas_call x1, Pallas kernels, shards(): pl.pallas_call(functools.partial(kernel, size), out_shape=tuple((pltpu.VM...  54.7 us

profile of v5, /device:TPU:1, one launch (start us, length us, event | category | flops | bytes accessed | tf_op | source)
XLA Modules:
  0.0 56.1 jit_solution(7048013533803698926)
XLA Ops:
  0.6 54.7 %block_sparse_ffn.1 = (bf16[8,1024]{1,0:T(8,128)(2,1)S(1)}, bf16[8,1024]{1,0:T(8,128)(2,1)S(1)}, f32[8,16,128]{2,1,0:T(8,128)S(1)}, f32[8,16,128]{2,1,0:T(8,128)S(1)}) custom-call(s32[8]{0:T(128)} %bitcast.10, s32[8]{0:T(128)} %bitcast.11, s32[8]{0:T(128)} %bitcast.12, s32[8]{0:T(128)} %bitcast.13, bf16[128,1024]{1,0:T(8,128)(2,1)} %tok_hbm.1, ...), custom_call_target="tpu_custom_call" | custom-call | tf_op jit(solution)/shard_map/block_sparse_ffn/pallas_call | solution.py:300
  55.4 0.7 %write_results.1 = (bf16[8,1024]{1,0:T(8,128)(2,1)}, bf16[8,1024]{1,0:T(8,128)(2,1)}, f32[8,16,128]{2,1,0:T(8,128)}, f32[8,16,128]{2,1,0:T(8,128)}) custom-call(bf16[8,1024]{1,0:T(8,128)(2,1)S(1)} %get-tuple-element.12.refs_0_, bf16[8,1024]{1,0:T(8,128)(2,1)S(1)} %get-tuple-element.13.refs_1_, f32[8,16,128]{2,1,0:T(8,128)S(1)} %get-tuple-element.14.refs_2_, ...), custom_call_target="tpu_custom_call" | custom-call | tf_op jit(solution)/shard_map/write_results/pallas_call | solution.py:339
